TPU v7x, 256 devices: a whole 4x4x8 slice. The times are simulated.
256 devices in a mesh: fsdp: 16 (over x_lo, z), expert: 16 (over y, x_hi, core).
Axes of the slice: x: 4 (x_hi: 2, x_lo: 2; x = x_hi * 2 + x_lo), y: 4, z: 8, core: 2. Of those that a mesh axis runs over, the one named last changes fastest.
Arguments:
- tokens: bfloat16 [2048, 3072], P('expert'), may hold values from -6 to 6
- cotangent: bfloat16 [2048, 3072], P('expert'), may hold values from -6 to 6
- expert_ids: int32 [2048, 4], P('expert'), may hold values from 0 to 15, all different within a row; in each aligned block of 128 rows (0 to 127, 128 to 255, ...) at most 40 rows name the same one
- gate_values: bfloat16 [2048, 4], P('expert'), may hold values from 0.049804688 to 0.5
- w_in: bfloat16 [3072, 16, 6144], P(None, 'expert', 'fsdp'), may hold values from -0.109375 to 0.109375
- w_out: bfloat16 [6144, 16, 3072], P('fsdp', 'expert'), may hold values from -0.078125 to 0.078125
Outputs:
- grad_tokens: bfloat16 [2048, 3072], P('expert')
- grad_gates: bfloat16 [2048, 4], P('expert')
- grad_w_in: bfloat16 [3072, 16, 6144], P(None, 'expert', 'fsdp')
- grad_w_out: bfloat16 [6144, 16, 3072], P('fsdp', 'expert')
Inputs may be any that keep to these rules, and one draw needn't show every extreme that they name: `expert_ids`: in each aligned block of 128 rows (the rows of one index of the expert axis) the 4 entries of a row differ, no expert is named by more than 40 rows, a bound that some block reaches.
All inputs are finite; a program needn't handle non-finite values.
Results may differ from a plain program's by a relative error of at most 0.0049.
Values may be sent and summed in bfloat16 or wider, within the bound.
A program may use at most 128 MiB of HBM per device.

v0:
```python
import jax
import jax.numpy as jnp
from jax import lax
from jax.sharding import PartitionSpec as P

EXPERTS = 16
CAP = 40
F32 = jnp.float32
BF16 = jnp.bfloat16


def local(tokens, cotangent, expert_ids, gate_values, w_in, w_out):
    rows, width = tokens.shape
    n_f = lax.axis_size("fsdp")
    part = 2 * width // n_f
    me_f = lax.axis_index("fsdp")
    half = me_f // (n_f // 2)
    col = me_f % (n_f // 2) * part
    ids_t = expert_ids.T
    experts = jnp.arange(EXPERTS, dtype=jnp.int32)[:, None]
    hit = ids_t[None] == experts[:, :, None]
    named = jnp.any(hit, axis=1)
    gates_of = jnp.sum(jnp.where(hit, gate_values.T[None].astype(F32), 0.0), axis=1)
    before = jnp.arange(rows)[:, None] < jnp.arange(rows)[None, :]
    place = jnp.dot(named.astype(BF16), before.astype(BF16), preferred_element_type=F32).astype(
        jnp.int32
    )
    slots = jnp.arange(CAP, dtype=jnp.int32)[None, :, None]
    pick = ((place[:, None, :] == slots) & named[:, None, :]).reshape(EXPERTS * CAP, rows)
    pick_b = pick.astype(BF16)
    gate_send = jnp.sum(
        jnp.where(pick.reshape(EXPERTS, CAP, rows), gates_of[:, None, :], 0.0), axis=2
    )
    chosen = jnp.where(
        half == 0,
        lax.dynamic_slice_in_dim(tokens, col, part, 1),
        lax.dynamic_slice_in_dim(cotangent, col, part, 1),
    )
    send = jnp.dot(pick_b, chosen, preferred_element_type=F32).astype(BF16)
    send = send.reshape(EXPERTS, CAP, part)
    got = lax.all_to_all(send, "expert", split_axis=0, concat_axis=0, tiled=True)
    gate_got = lax.all_to_all(gate_send, "expert", split_axis=0, concat_axis=0, tiled=True)
    every = lax.all_gather(got.reshape(EXPERTS * CAP, part), "fsdp", axis=0)
    xs, gs = (every[: n_f // 2], every[n_f // 2 :])
    win = w_in.reshape(n_f // 2, part, -1)
    wout = w_out.reshape(-1, n_f // 2, part)
    pre = jnp.einsum("zsd,zdf->sf", xs, win, preferred_element_type=F32)
    up = jnp.einsum("zsd,fzd->sf", gs, wout, preferred_element_type=F32)
    gate = gate_got.reshape(EXPERTS * CAP, 1)
    squash = jax.nn.sigmoid(pre)
    active = pre * squash
    gate_part = jnp.sum(active * up, axis=-1)
    act_gated = (gate * active).astype(BF16)
    grad_pre = (gate * squash * (1.0 + pre * (1.0 - squash)) * up).astype(BF16)
    w16 = w_in.reshape(n_f, width // n_f, -1)
    part_x = jnp.einsum("sf,zdf->zsd", grad_pre, w16, preferred_element_type=F32)
    mine = lax.psum_scatter(part_x, "fsdp", scatter_dimension=0, tiled=False)
    gate_sum = lax.psum(gate_part.reshape(EXPERTS, CAP), "fsdp")
    back_x = lax.all_to_all(mine.reshape(EXPERTS, CAP, -1), "expert", 0, 0, tiled=True)
    back_gate = lax.all_to_all(gate_sum, "expert", split_axis=0, concat_axis=0, tiled=True)
    grad_in = jnp.einsum("zsd,sf->zdf", xs, grad_pre, preferred_element_type=F32).astype(BF16)
    grad_out = jnp.einsum("sf,zsd->fzd", act_gated, gs, preferred_element_type=F32).astype(BF16)
    tok = jnp.dot(
        pick.astype(F32).T,
        back_x.reshape(EXPERTS * CAP, -1),
        precision=lax.Precision.HIGHEST,
        preferred_element_type=F32,
    ).astype(BF16)
    grad_tokens = lax.all_gather(tok, "fsdp", axis=1, tiled=True)
    by_expert = jnp.sum(
        jnp.where(pick.reshape(EXPERTS, CAP, rows), back_gate[:, :, None], 0.0), axis=1
    )
    grad_gates = jnp.sum(jnp.where(hit, by_expert[:, None, :], 0.0), axis=0).T.astype(BF16)
    return (grad_tokens, grad_gates, grad_in.reshape(w_in.shape), grad_out.reshape(w_out.shape))


def solution(mesh):
    return jax.shard_map(
        local,
        mesh=mesh,
        in_specs=(
            P("expert", None),
            P("expert", None),
            P("expert", None),
            P("expert", None),
            P(None, "expert", "fsdp"),
            P("fsdp", "expert", None),
        ),
        out_specs=(
            P("expert", None),
            P("expert", None),
            P(None, "expert", "fsdp"),
            P("fsdp", "expert", None),
        ),
        check_vma=False,
    )
```

profile of v0, /device:TPU:2, one launch (start us, length us, event | category | flops | bytes accessed | tf_op | source)
XLA Modules:
  0.0 350.6 jit_solution(9001200368042260039)
XLA Ops:
  7.2 0.0 copy-start
  7.2 0.0 copy-start.4
  7.2 0.0 all-gather.2.cloned.1.call-start
  7.3 0.8 fusion.27
  8.1 0.1 convolution_convert_fusion.2
  8.2 0.1 eq.50
  8.3 0.2 fusion.19
  8.5 1.2 convolution_convert_fusion.1
  9.7 18.0 %all_to_all.28 = bf16[16,40,384]{2,1,0:T(8,128)(2,1)} all-to-all(bf16[16,40,384]{2,1,0:T(8,128)(2,1)S(1)} %bitcast.59), channel_id=1, replica_groups=mesh['fsdp'=16,'expert'=16] {'expert'}, dimensions={0} | all-to-all | bytes 983040 | tf_op jit(solution)/shard_map/all_to_all | solution.py:41
  27.8 0.0 all-gather.2.cloned.1.call-update
  27.8 3.6 %copy.59 = bf16[48,8,8,384]{3,2,1,0:T(8,128)(2,1)} copy(bf16[48,8,8,384]{3,1,2,0:T(8,128)(2,1)} %bitcast.55) | data formatting | bytes 4718592
  31.4 0.0 copy-done.4
  31.4 90.4 %all-gather.2.cloned.1.call-done = bf16[16,640,384]{2,1,0:T(8,128)(2,1)} async-done(((bf16[1,640,384]{2,1,0:T(8,128)(2,1)}), bf16[16,640,384]{2,1,0:T(8,128)(2,1)}) %all-gather.2.cloned.1.call-update) | async-done | bytes 7864336 | tf_op jit(solution)/shard_map/all_gather | solution.py:43
  121.8 0.0 copy-done
  121.8 0.0 copy-start.1
  121.8 0.0 copy-start.5
  121.8 4.3 %convolution_bitcast_fusion.1 = f32[640,384]{0,1:T(8,128)S(1)} fusion(bf16[16,640,384]{2,1,0:T(8,128)(2,1)} %all-gather.2.cloned.1.call-done, bf16[8,384,384]{2,1,0:T(8,128)(2,1)S(1)} %bitcast.53), kind=kOutput, calls=%fused_computation.8 | convolution fusion | flops 1509949440 | bytes 11206656 | tf_op jit(solution)/shard_map/zsd,zdf->sf/dot_general | solution.py:47
  126.1 0.0 copy-start.2
  126.1 0.0 copy-done.1
  126.1 0.8 copy-done.5
  127.0 0.0 copy-start.3
  127.0 3.0 multiply_reduce_fusion
  129.9 0.0 copy-done.2
  129.9 0.1 all_to_all.22
  130.0 33.5 %psum.7 = f32[16,1,40]{2,1,0:T(1,128)} all-reduce(f32[16,1,40]{2,1,0:T(1,128)S(1)} %all_to_all.22), channel_id=1, replica_groups=mesh['fsdp'=16,'expert'=16] {'fsdp'}, use_global_device_ids=true, to_apply=%region_5.6 | all-reduce | flops 640 | bytes 5120 | tf_op jit(solution)/shard_map/psum | solution.py:58
  163.5 6.2 %all-to-all-start.3 = ((f32[16,1,40]{2,1,0:T(1,128)}), f32[16,1,40]{2,1,0:T(1,128)S(1)}, u32[]{:S(2)}, u32[]{:S(2)}) async-start(f32[16,1,40]{2,1,0:T(1,128)} %psum.7), calls=%async_computation.4 | async-start | bytes 16384 | tf_op jit(solution)/shard_map/all_to_all | solution.py:60
  169.7 0.0 reduce-scatter.2.cloned.1.call-start
  169.8 0.0 copy-done.3
  169.8 7.4 %all-to-all-done.3 = f32[16,1,40]{2,1,0:T(1,128)S(1)} async-done(((f32[16,1,40]{2,1,0:T(1,128)}), f32[16,1,40]{2,1,0:T(1,128)S(1)}, u32[]{:S(2)}, u32[]{:S(2)}) %all-to-all-start.3) | async-done | bytes 2592 | tf_op jit(solution)/shard_map/all_to_all | solution.py:60
  177.2 0.3 select_reduce_fusion
  177.5 10.1 %all_to_all.29 = f32[16,1,40]{2,1,0:T(1,128)S(1)} all-to-all(f32[16,1,40]{2,1,0:T(1,128)S(1)} %bitcast.61), channel_id=1, replica_groups=mesh['fsdp'=16,'expert'=16] {'expert'}, dimensions={0} | all-to-all | bytes 5120 | tf_op jit(solution)/shard_map/all_to_all | solution.py:42
  187.6 0.5 broadcast.26
  188.1 0.7 reduce.3
  188.8 0.1 mul.34
  188.9 1.9 multiply_convert_fusion.1
  190.8 4.6 %convolution_bitcast_fusion = f32[16,640,192]{1,2,0:T(8,128)} fusion(bf16[16,192,384]{2,1,0:T(8,128)(2,1)S(1)} %bitcast.52, bf16[640,384]{0,1:T(8,128)(2,1)S(1)} %multiply_convert_fusion.1), kind=kOutput, calls=%fused_computation.2 | convolution fusion | flops 1509949440 | bytes 10715136 | tf_op jit(solution)/shard_map/sf,zdf->zsd/dot_general | solution.py:56
  195.3 0.0 reduce-scatter.2.cloned.1.call-update
  195.4 0.6 select_reduce_fusion.2
  196.0 6.3 %fusion.4 = bf16[384,8,384]{0,2,1:T(8,128)(2,1)} fusion(bf16[16,640,384]{2,1,0:T(8,128)(2,1)} %all-gather.2.cloned.1.call-done, f32[640]{0:T(1024)S(1)} %mul.34, f32[640,384]{0,1:T(8,128)} %copy-done.2), kind=kOutput, calls=%fused_computation.5 | convolution fusion | flops 1512603648 | bytes 7277056 | tf_op jit(solution)/shard_map/sf,zsd->fzd/dot_general | solution.py:62
  202.3 4.3 %copy.49 = bf16[384,1,3072]{2,0,1:T(8,128)(2,1)} copy(bf16[384,1,3072]{0,2,1:T(8,128)(2,1)} %bitcast.57) | data formatting | bytes 4718592
  206.5 77.1 %reduce-scatter.2.cloned.1.call-done = f32[1,640,192]{1,2,0:T(8,128)} async-done(((f32[16,640,192]{1,2,0:T(8,128)}), f32[1,640,192]{1,2,0:T(8,128)}) %reduce-scatter.2.cloned.1.call-update) | async-done | bytes 491536 | tf_op jit(solution)/shard_map/reduce_scatter | solution.py:57
  283.6 2.1 copy.43
  285.7 6.2 %all-to-all-start.2 = ((f32[16,40,192]{2,1,0:T(8,128)}), f32[16,40,192]{2,1,0:T(8,128)S(1)}, u32[]{:S(2)}, u32[]{:S(2)}) async-start(f32[16,40,192]{2,1,0:T(8,128)} %bitcast.54), calls=%async_computation.3 | async-start | bytes 1310720 | tf_op jit(solution)/shard_map/all_to_all | solution.py:59
  291.9 6.0 %convolution_convert_fusion = bf16[8,384,384]{2,1,0:T(8,128)(2,1)} fusion(bf16[16,640,384]{2,1,0:T(8,128)(2,1)} %all-gather.2.cloned.1.call-done, bf16[640,384]{0,1:T(8,128)(2,1)S(1)} %multiply_convert_fusion.1), kind=kOutput, calls=%fused_computation.6 | convolution fusion | flops 1511129088 | bytes 10715136 | tf_op jit(solution)/shard_map/zsd,sf->zdf/dot_general | solution.py:61
  297.9 7.8 %all-to-all-done.2 = f32[16,40,192]{2,1,0:T(8,128)S(1)} async-done(((f32[16,40,192]{2,1,0:T(8,128)}), f32[16,40,192]{2,1,0:T(8,128)S(1)}, u32[]{:S(2)}, u32[]{:S(2)}) %all-to-all-start.2) | async-done | bytes 491552 | tf_op jit(solution)/shard_map/all_to_all | solution.py:59
  305.7 0.7 fusion.10
  306.4 36.2 %all_gather.7 = bf16[128,3072]{0,1:T(8,128)(2,1)S(1)} all-gather(bf16[128,192]{0,1:T(8,128)(2,1)S(1)} %fusion.10), channel_id=1, replica_groups=mesh['fsdp'=16,'expert'=16] {'fsdp'}, dimensions={1}, use_global_device_ids=true | all-gather | bytes 835584 | tf_op jit(solution)/shard_map/all_gather | solution.py:69
  342.6 1.2 copy.48
  (3 shorter events, 0.0 us)
Async XLA Ops:
  7.2 114.7 %copy-start = (bf16[3072,1,384]{2,0,1:T(8,128)(2,1)S(1)}, bf16[3072,1,384]{2,0,1:T(8,128)(2,1)}, u32[]{:S(2)}) copy-start(bf16[3072,1,384]{2,0,1:T(8,128)(2,1)} %param.10) | copy-start | bytes 7077892
  7.2 24.2 %copy-start.4 = (bf16[128,4]{0,1:T(4,128)(2,1)S(1)}, bf16[128,4]{0,1:T(4,128)(2,1)}, u32[]{:S(2)}) copy-start(bf16[128,4]{0,1:T(4,128)(2,1)} %param.9) | copy-start | bytes 3076
  7.2 114.6 %all-gather.2.cloned.1.call-start = ((), (), s32[]{:S(2)}) async-start(), calls=%async_computation.5 | async-start | bytes 8355840 | tf_op jit(solution)/shard_map/all_gather | solution.py:43
  121.8 4.3 %copy-start.1 = (bf16[48,8,8,384]{3,2,1,0:T(8,128)(2,1)S(1)}, bf16[48,8,8,384]{3,2,1,0:T(8,128)(2,1)}, u32[]{:S(2)}) copy-start(bf16[48,8,8,384]{3,2,1,0:T(8,128)(2,1)} %copy.59) | copy-start | bytes 7077892
  121.8 5.1 %copy-start.5 = (bf16[16,640,384]{2,1,0:T(8,128)(2,1)S(1)}, bf16[16,640,384]{2,1,0:T(8,128)(2,1)}, u32[]{:S(2)}) copy-start(bf16[16,640,384]{2,1,0:T(8,128)(2,1)} %all-gather.2.cloned.1.call-done) | copy-start | bytes 23592964
  126.1 3.8 %copy-start.2 = (f32[640,384]{0,1:T(8,128)}, f32[640,384]{0,1:T(8,128)S(1)}, u32[]{:S(2)}) copy-start(f32[640,384]{0,1:T(8,128)S(1)} %convolution_bitcast_fusion.1) | copy-start | bytes 2949124
  127.0 42.8 %copy-start.3 = (s32[128,4]{0,1:T(4,128)S(1)}, s32[128,4]{0,1:T(4,128)}, u32[]{:S(2)}) copy-start(s32[128,4]{0,1:T(4,128)} %param.8) | copy-start | bytes 6148
  163.5 13.7 %all-to-all-start.3 = ((f32[16,1,40]{2,1,0:T(1,128)}), f32[16,1,40]{2,1,0:T(1,128)S(1)}, u32[]{:S(2)}, u32[]{:S(2)}) async-start(f32[16,1,40]{2,1,0:T(1,128)} %psum.7), calls=%async_computation.4 | async-start | bytes 16384 | tf_op jit(solution)/shard_map/all_to_all | solution.py:60
  169.7 113.9 %reduce-scatter.2.cloned.1.call-start = ((), (), s32[]{:S(2)}) async-start(), calls=%async_computation.6 | async-start | bytes 8355840 | tf_op jit(solution)/shard_map/reduce_scatter | solution.py:57
  285.7 20.0 %all-to-all-start.2 = ((f32[16,40,192]{2,1,0:T(8,128)}), f32[16,40,192]{2,1,0:T(8,128)S(1)}, u32[]{:S(2)}, u32[]{:S(2)}) async-start(f32[16,40,192]{2,1,0:T(8,128)} %bitcast.54), calls=%async_computation.3 | async-start | bytes 1310720 | tf_op jit(solution)/shard_map/all_to_all | solution.py:59
Sparse Core Ops, SparseCore 0:
  27.9 93.8 all-gather.1
  195.5 88.0 reduce-scatter.1
where the time goes:
time: 351 us
  waiting for transfers between devices  183 us (52%)
  blocking collectives  97.8 us (28%)
  matrix products  26.2 us (7%)
  between operations  14.2 us (4%)
  local copies, waits for them, and re-layouts  12.7 us (4%)
  starting transfers between devices  12.5 us (4%)
  other arithmetic  4.41 us (1%)
    all_gather x1, waiting for transfers between devices, local(): every = lax.all_gather(got.reshape(EXPERTS * CAP, part), 'fsdp', axis=0)  90.4 us
    reduce_scatter x1, waiting for transfers between devices, local(): mine = lax.psum_scatter(part_x, 'fsdp', scatter_dimension=0, tiled=False)  77.1 us
    all_gather x1, blocking collectives, local(): grad_tokens = lax.all_gather(tok, 'fsdp', axis=1, tiled=True)  36.2 us
    psum x1, blocking collectives, local(): gate_sum = lax.psum(gate_part.reshape(EXPERTS, CAP), 'fsdp')  33.5 us
    all_to_all x1, blocking collectives, local(): lax.all_to_all(send, 'expert', split_axis=0, concat_axis=0, tiled=True)  18 us
    all_to_all x1, blocking collectives, local(): lax.all_to_all(gate_send, 'expert', split_axis=0, concat_axis=0, tiled=True)  10.1 us
    unnamed x15, local copies, waits for them, and re-layouts  9.86 us
    all_to_all x1, waiting for transfers between devices, local(): lax.all_to_all(mine.reshape(EXPERTS, CAP, -1), 'expert', 0, 0, tiled=True)  7.79 us
  transfers between devices with their start and end apart: 4, of which 4 were waited for; matrix products, arithmetic and copies ran while one was open for 6% of the time, Pallas kernels for 0%

commit v1 on v0

--- a/solution.py
+++ b/solution.py
@@ -66,7 +66,9 @@
         precision=lax.Precision.HIGHEST,
         preferred_element_type=F32,
     ).astype(BF16)
-    grad_tokens = lax.all_gather(tok, "fsdp", axis=1, tiled=True)
+    grad_tokens = jnp.concatenate(
+        lax.all_to_all(jnp.stack([tok] * lax.axis_size("fsdp")), "fsdp", 0, 0), axis=1
+    )
     by_expert = jnp.sum(
         jnp.where(pick.reshape(EXPERTS, CAP, rows), back_gate[:, :, None], 0.0), axis=1
     )

time: 351 us -> 342 us (0.974)
  blocking collectives: 97.8 us -> 81.4 us
  waiting for transfers between devices: 183 us -> 189 us
    all_gather x1 -> x0, blocking collectives: 36.2 us -> none  [local(): grad_tokens = lax.all_gather(tok, 'fsdp', axis=1, tiled=True)]
    all_to_all x0 -> x1, blocking collectives: none -> 19.8 us  [local(): lax.all_to_all(mine.reshape(EXPERTS, CAP, -1), 'expert', 0, 0, tiled=True)]
    reduce_scatter x1, waiting for transfers between devices: 77.1 us -> 88.2 us  [local(): mine = lax.psum_scatter(part_x, 'fsdp', scatter_dimension=0, tiled=False)]
    all_to_all x1, waiting for transfers between devices: 7.79 us -> 2.52 us  [local(): lax.all_to_all(jnp.stack([tok] * lax.axis_size('fsdp')), 'fsdp', 0, 0)]
    unnamed x15 -> x17, local copies, waits for them, and re-layouts: 9.86 us -> 10.6 us
where the time goes in v1:
time: 342 us; the launch traced here: 340 us
  waiting for transfers between devices  189 us (55%)
  blocking collectives  81.4 us (24%)
  matrix products  26.3 us (8%)
  between operations  14.2 us (4%)
  local copies, waits for them, and re-layouts  13.7 us (4%)
  starting transfers between devices  12 us (4%)
  other arithmetic  4.11 us (1%)
    all_gather x1, waiting for transfers between devices, local(): every = lax.all_gather(got.reshape(EXPERTS * CAP, part), 'fsdp', axis=0)  90.4 us
    reduce_scatter x1, waiting for transfers between devices, local(): mine = lax.psum_scatter(part_x, 'fsdp', scatter_dimension=0, tiled=False)  88.2 us
    psum x1, blocking collectives, local(): gate_sum = lax.psum(gate_part.reshape(EXPERTS, CAP), 'fsdp')  33.5 us
    all_to_all x1, blocking collectives, local(): lax.all_to_all(mine.reshape(EXPERTS, CAP, -1), 'expert', 0, 0, tiled=True)  19.8 us
    all_to_all x1, blocking collectives, local(): lax.all_to_all(send, 'expert', split_axis=0, concat_axis=0, tiled=True)  18 us
    unnamed x17, local copies, waits for them, and re-layouts  10.6 us
    all_to_all x1, blocking collectives, local(): lax.all_to_all(gate_send, 'expert', split_axis=0, concat_axis=0, tiled=True)  10.1 us
    all_to_all x1, waiting for transfers between devices, local(): lax.all_to_all(gate_sum, 'expert', split_axis=0, concat_axis=0, tiled=True)  7.43 us
  transfers between devices with their start and end apart: 4, of which 4 were waited for; matrix products, arithmetic and copies ran while one was open for 6% of the time, Pallas kernels for 0%

profile of v1, /device:TPU:2, one launch (start us, length us, event | category | flops | bytes accessed | tf_op | source)
XLA Modules:
  0.0 340.4 jit_solution(2988691049170488927)
XLA Ops:
  7.2 0.0 copy-start
  7.2 0.0 copy-start.5
  7.2 0.0 all-gather.2.cloned.1.call-start
  7.3 0.8 fusion.27
  8.1 0.1 convolution_convert_fusion.2
  8.2 0.1 eq.50
  8.3 0.2 fusion.19
  8.5 1.2 convolution_convert_fusion.1
  9.7 18.0 %all_to_all.33 = bf16[16,40,384]{2,1,0:T(8,128)(2,1)} all-to-all(bf16[16,40,384]{2,1,0:T(8,128)(2,1)S(1)} %bitcast.63), channel_id=1, replica_groups=mesh['fsdp'=16,'expert'=16] {'expert'}, dimensions={0} | all-to-all | bytes 983040 | tf_op jit(solution)/shard_map/all_to_all | solution.py:41
  27.8 0.0 all-gather.2.cloned.1.call-update
  27.8 3.6 %copy.59 = bf16[48,8,8,384]{3,2,1,0:T(8,128)(2,1)} copy(bf16[48,8,8,384]{3,1,2,0:T(8,128)(2,1)} %bitcast.59) | data formatting | bytes 4718592
  31.4 0.0 copy-done.5
  31.4 90.4 %all-gather.2.cloned.1.call-done = bf16[16,640,384]{2,1,0:T(8,128)(2,1)} async-done(((bf16[1,640,384]{2,1,0:T(8,128)(2,1)}), bf16[16,640,384]{2,1,0:T(8,128)(2,1)}) %all-gather.2.cloned.1.call-update) | async-done | bytes 7864336 | tf_op jit(solution)/shard_map/all_gather | solution.py:43
  121.8 0.0 copy-done
  121.8 4.3 %convolution_bitcast_fusion.1 = f32[640,384]{0,1:T(8,128)S(1)} fusion(bf16[16,640,384]{2,1,0:T(8,128)(2,1)} %all-gather.2.cloned.1.call-done, bf16[8,384,384]{2,1,0:T(8,128)(2,1)S(1)} %bitcast.56), kind=kOutput, calls=%fused_computation.8 | convolution fusion | flops 1509949440 | bytes 11206656 | tf_op jit(solution)/shard_map/zsd,zdf->sf/dot_general | solution.py:47
  126.1 0.0 copy-start.3
  126.1 0.0 copy-done.1
  126.1 0.8 copy-done.6
  127.0 3.0 multiply_reduce_fusion
  129.9 0.1 all_to_all.26
  130.0 33.5 %psum.7 = f32[16,1,40]{2,1,0:T(1,128)} all-reduce(f32[16,1,40]{2,1,0:T(1,128)S(1)} %all_to_all.26), channel_id=1, replica_groups=mesh['fsdp'=16,'expert'=16] {'fsdp'}, use_global_device_ids=true, to_apply=%region_5.6 | all-reduce | flops 640 | bytes 5120 | tf_op jit(solution)/shard_map/psum | solution.py:58
  163.5 6.2 %all-to-all-start.4 = ((f32[16,1,40]{2,1,0:T(1,128)}), f32[16,1,40]{2,1,0:T(1,128)S(1)}, u32[]{:S(2)}, u32[]{:S(2)}) async-start(f32[16,1,40]{2,1,0:T(1,128)} %psum.7), calls=%async_computation.5 | async-start | bytes 16384 | tf_op jit(solution)/shard_map/all_to_all | solution.py:60
  169.7 0.0 reduce-scatter.2.cloned.1.call-start
  169.8 0.0 copy-done.4
  169.8 7.4 %all-to-all-done.4 = f32[16,1,40]{2,1,0:T(1,128)S(1)} async-done(((f32[16,1,40]{2,1,0:T(1,128)}), f32[16,1,40]{2,1,0:T(1,128)S(1)}, u32[]{:S(2)}, u32[]{:S(2)}) %all-to-all-start.4) | async-done | bytes 2592 | tf_op jit(solution)/shard_map/all_to_all | solution.py:60
  177.2 0.3 select_reduce_fusion
  177.5 10.1 %all_to_all.34 = f32[16,1,40]{2,1,0:T(1,128)S(1)} all-to-all(f32[16,1,40]{2,1,0:T(1,128)S(1)} %bitcast.65), channel_id=1, replica_groups=mesh['fsdp'=16,'expert'=16] {'expert'}, dimensions={0} | all-to-all | bytes 5120 | tf_op jit(solution)/shard_map/all_to_all | solution.py:42
  187.6 0.5 broadcast.28
  188.1 0.7 reduce.3
  188.8 0.1 mul.34
  188.9 0.0 copy-done.3
  188.9 1.6 multiply_convert_fusion.1
  190.5 0.0 copy-start.2
  190.5 0.8 copy-done.2
  191.3 4.5 %convolution_bitcast_fusion = f32[16,640,192]{1,2,0:T(8,128)} fusion(bf16[16,192,384]{2,1,0:T(8,128)(2,1)S(1)} %bitcast.55, bf16[640,384]{0,1:T(8,128)(2,1)S(1)} %multiply_convert_fusion.1), kind=kOutput, calls=%fused_computation.2 | convolution fusion | flops 1509949440 | bytes 10715136 | tf_op jit(solution)/shard_map/sf,zdf->zsd/dot_general | solution.py:56
  195.8 0.0 reduce-scatter.2.cloned.1.call-update
  195.8 88.2 %reduce-scatter.2.cloned.1.call-done = f32[1,640,192]{1,2,0:T(8,128)} async-done(((f32[16,640,192]{1,2,0:T(8,128)}), f32[1,640,192]{1,2,0:T(8,128)}) %reduce-scatter.2.cloned.1.call-update) | async-done | bytes 491536 | tf_op jit(solution)/shard_map/reduce_scatter | solution.py:57
  284.1 1.3 copy.43
  285.3 19.8 %all_to_all.35 = f32[16,40,192]{2,1,0:T(8,128)S(1)} all-to-all(f32[16,40,192]{2,1,0:T(8,128)S(1)} %bitcast.58), channel_id=1, replica_groups=mesh['fsdp'=16,'expert'=16] {'expert'}, dimensions={0} | all-to-all | bytes 983040 | tf_op jit(solution)/shard_map/all_to_all | solution.py:59
  305.1 0.7 fusion.10
  305.8 1.0 stack.2
  306.9 5.7 %all-to-all-start.3 = ((bf16[16,128,192]{1,2,0:T(8,128)(2,1)}), bf16[16,128,192]{1,2,0:T(8,128)(2,1)S(1)}, u32[]{:S(2)}, u32[]{:S(2)}) async-start(bf16[16,128,192]{1,2,0:T(8,128)(2,1)} %stack.2), calls=%async_computation.4 | async-start | bytes 1572864 | tf_op jit(solution)/shard_map/all_to_all | solution.py:70
  312.6 0.6 select_reduce_fusion.2
  313.2 6.3 %fusion.4 = bf16[384,8,384]{0,2,1:T(8,128)(2,1)} fusion(bf16[16,640,384]{2,1,0:T(8,128)(2,1)} %all-gather.2.cloned.1.call-done, f32[640]{0:T(1024)S(1)} %mul.34, f32[640,384]{0,1:T(8,128)} %copy-done.3), kind=kOutput, calls=%fused_computation.5 | convolution fusion | flops 1512603648 | bytes 7277056 | tf_op jit(solution)/shard_map/sf,zsd->fzd/dot_general | solution.py:62
  319.5 4.3 %copy.49 = bf16[384,1,3072]{2,0,1:T(8,128)(2,1)} copy(bf16[384,1,3072]{0,2,1:T(8,128)(2,1)} %bitcast.61) | data formatting | bytes 4718592
  323.7 6.1 %convolution_convert_fusion = bf16[8,384,384]{2,1,0:T(8,128)(2,1)} fusion(bf16[16,640,384]{2,1,0:T(8,128)(2,1)} %all-gather.2.cloned.1.call-done, bf16[640,384]{0,1:T(8,128)(2,1)} %copy-done.2), kind=kOutput, calls=%fused_computation.6 | convolution fusion | flops 1511129088 | bytes 10715136 | tf_op jit(solution)/shard_map/zsd,sf->zdf/dot_general | solution.py:61
  329.8 2.5 all-to-all-done.3
  332.4 1.2 copy.48
  (6 shorter events, 0.0 us)
Async XLA Ops:
  7.2 114.7 %copy-start = (bf16[3072,1,384]{2,0,1:T(8,128)(2,1)S(1)}, bf16[3072,1,384]{2,0,1:T(8,128)(2,1)}, u32[]{:S(2)}) copy-start(bf16[3072,1,384]{2,0,1:T(8,128)(2,1)} %param.10) | copy-start | bytes 7077892
  7.2 24.2 %copy-start.5 = (bf16[128,4]{0,1:T(4,128)(2,1)S(1)}, bf16[128,4]{0,1:T(4,128)(2,1)}, u32[]{:S(2)}) copy-start(bf16[128,4]{0,1:T(4,128)(2,1)} %param.9) | copy-start | bytes 3076
  7.2 114.6 %all-gather.2.cloned.1.call-start = ((), (), s32[]{:S(2)}) async-start(), calls=%async_computation.6 | async-start | bytes 8355840 | tf_op jit(solution)/shard_map/all_gather | solution.py:43
  121.8 4.3 %copy-start.1 = (bf16[48,8,8,384]{3,2,1,0:T(8,128)(2,1)S(1)}, bf16[48,8,8,384]{3,2,1,0:T(8,128)(2,1)}, u32[]{:S(2)}) copy-start(bf16[48,8,8,384]{3,2,1,0:T(8,128)(2,1)} %copy.59) | copy-start | bytes 7077892
  121.8 5.1 %copy-start.6 = (bf16[16,640,384]{2,1,0:T(8,128)(2,1)S(1)}, bf16[16,640,384]{2,1,0:T(8,128)(2,1)}, u32[]{:S(2)}) copy-start(bf16[16,640,384]{2,1,0:T(8,128)(2,1)} %all-gather.2.cloned.1.call-done) | copy-start | bytes 23592964
  126.1 62.8 %copy-start.3 = (f32[640,384]{0,1:T(8,128)}, f32[640,384]{0,1:T(8,128)S(1)}, u32[]{:S(2)}) copy-start(f32[640,384]{0,1:T(8,128)S(1)} %convolution_bitcast_fusion.1) | copy-start | bytes 2949124
  127.0 42.8 %copy-start.4 = (s32[128,4]{0,1:T(4,128)S(1)}, s32[128,4]{0,1:T(4,128)}, u32[]{:S(2)}) copy-start(s32[128,4]{0,1:T(4,128)} %param.8) | copy-start | bytes 6148
  163.5 13.7 %all-to-all-start.4 = ((f32[16,1,40]{2,1,0:T(1,128)}), f32[16,1,40]{2,1,0:T(1,128)S(1)}, u32[]{:S(2)}, u32[]{:S(2)}) async-start(f32[16,1,40]{2,1,0:T(1,128)} %psum.7), calls=%async_computation.5 | async-start | bytes 16384 | tf_op jit(solution)/shard_map/all_to_all | solution.py:60
  169.7 114.4 %reduce-scatter.2.cloned.1.call-start = ((), (), s32[]{:S(2)}) async-start(), calls=%async_computation.7 | async-start | bytes 8355840 | tf_op jit(solution)/shard_map/reduce_scatter | solution.py:57
  190.5 0.8 copy-start.2
  306.9 25.5 %all-to-all-start.3 = ((bf16[16,128,192]{1,2,0:T(8,128)(2,1)}), bf16[16,128,192]{1,2,0:T(8,128)(2,1)S(1)}, u32[]{:S(2)}, u32[]{:S(2)}) async-start(bf16[16,128,192]{1,2,0:T(8,128)(2,1)} %stack.2), calls=%async_computation.4 | async-start | bytes 1572864 | tf_op jit(solution)/shard_map/all_to_all | solution.py:70
Sparse Core Ops, SparseCore 0:
  27.9 93.8 all-gather.1
  196.0 88.0 reduce-scatter.1
